TPU v7x, 256 devices: a whole 4x4x8 slice. The times are simulated.
256 devices in a mesh: half: 2 (over core), row: 8 (over z_hi, x), col: 16 (over y, z_lo).
Axes of the slice: x: 4, y: 4, z: 8 (z_hi: 2, z_lo: 4; z = z_hi * 4 + z_lo), core: 2. Of those that a mesh axis runs over, the one named last changes fastest.
Arguments:
- parent_front: float32 [16384, 16384], P(('half', 'row'), 'col'), may hold values from -6 to 6
- child_blocks: float32 [2, 8192, 8192], P('half', 'row', 'col'), may hold values from -6 to 6
- row_maps: int32 [2, 8192], replicated, may hold values from 0 to 16383, as said below
- inverse_blocks: float32 [4, 128, 128], replicated, may hold values from -0.12 to 0.12
Outputs:
- updated_front: float32 [16384, 16384], P(('half', 'row'), 'col')
- panel_factor: bfloat16 [16384, 512], P(('half', 'row'))
Inputs may be any that keep to these rules, and one draw needn't show every extreme that they name: `row_maps`: each row lists 8192 distinct parent rows. In every aligned block of 512 entries of a row, at most 64 entries fall in one aligned block of 1024 parent rows, and that bound is reached in every such block; in every aligned block of 1024 entries, at most 128 fall in one aligned block of 1024 parent rows, and that bound is reached in every such block.
All inputs are finite; a program needn't handle non-finite values.
Results may differ from a plain program's by a relative error of at most 0.001.
Values sent between devices are 32-bit elements; how exact they have to be, the bound alone decides.
A program may use at most 128 MiB of HBM per device.

v0:
```python
import jax
import jax.numpy as jnp
from jax import lax
from jax.sharding import PartitionSpec as P


def from_root(block, axis, holder):
    block = jnp.where(lax.axis_index(axis) == holder, block, jnp.zeros_like(block))
    return lax.psum(block, axis)


def highest_outer(left, right):
    return lax.dot_general(
        left,
        right,
        (((1,), (1,)), ((), ())),
        precision=lax.Precision.HIGHEST,
        preferred_element_type=jnp.float32,
    )


def ranks(targets, count):
    onehot = (targets[..., None] == jnp.arange(count, dtype=jnp.int32)).astype(jnp.int32)
    before = jnp.cumsum(onehot, axis=-2) - onehot
    return jnp.sum(before * onehot, axis=-1)


def row_tables(row_maps, row_loc, groups, cap_rows, my_group):
    parent_rows = row_maps.reshape(groups, -1)
    targets = parent_rows // row_loc
    slots = ranks(targets, groups)
    sources = jnp.arange(groups, dtype=jnp.int32)[:, None]
    where_at = jnp.where(targets == my_group, sources * cap_rows + slots, groups * cap_rows)
    table = (
        jnp.full((groups * cap_rows,), row_loc, jnp.int32)
        .at[where_at.reshape(-1)]
        .set((parent_rows % row_loc).reshape(-1), mode="drop")
    )
    send_at = targets[my_group] * cap_rows + slots[my_group]
    return (send_at, table)


def col_tables(row_maps, col_loc, n_col, cap_cols, my_col):
    parent_cols = row_maps.reshape(2, n_col, -1)
    targets = parent_cols // col_loc
    slots = ranks(targets, n_col)
    sources = jnp.arange(n_col, dtype=jnp.int32)[None, :, None]
    where_at = jnp.where(targets == my_col, sources * cap_cols + slots, n_col * cap_cols)
    child_index = jnp.broadcast_to(jnp.arange(2, dtype=jnp.int32)[:, None, None], where_at.shape)
    table = (
        jnp.full((2, n_col * cap_cols), col_loc, jnp.int32)
        .at[child_index, where_at]
        .set(parent_cols % col_loc, mode="drop")
    )
    send_at = targets[:, my_col] * cap_cols + slots[:, my_col]
    return (send_at, table)


def row_pack(values, send_at, total):
    return jnp.zeros((total, values.shape[1]), values.dtype).at[send_at].set(values)


def col_pack(values, send_at, total):
    return jnp.zeros((values.shape[0], total), values.dtype).at[:, send_at].set(values)


def local(parent_front, child_blocks, row_maps, inverse_blocks):
    row_loc, col_loc = parent_front.shape
    child_rows, child_cols = (child_blocks.shape[1], child_blocks.shape[2])
    n_row = lax.axis_size("row")
    n_col = lax.axis_size("col")
    groups = lax.axis_size("half") * n_row
    my_child = lax.axis_index("half")
    my_group = my_child * n_row + lax.axis_index("row")
    my_col = lax.axis_index("col")
    cap_cols = 2 * child_cols // n_col
    cap_rows = n_col // n_row * (child_cols // groups + child_cols // n_col)
    slab_rows = n_row * cap_rows
    row_send, row_table = row_tables(row_maps, row_loc, groups, cap_rows, my_group)
    col_send, col_table = col_tables(row_maps, col_loc, n_col, cap_cols, my_col)
    mine = child_blocks[0]
    moved = row_pack(mine, row_send, groups * cap_rows)
    arrived = lax.all_to_all(
        moved, ("half", "row"), split_axis=0, concat_axis=0, tiled=True
    ).reshape(2, slab_rows, child_cols)
    outgoing = jnp.stack(
        [col_pack(arrived[child], col_send[child], n_col * cap_cols) for child in range(2)]
    )
    landed = lax.all_to_all(outgoing, "col", split_axis=2, concat_axis=2, tiled=True)
    row_dest = row_table.reshape(2, slab_rows)
    assembled = parent_front
    for child in range(2):
        spread = (
            jnp.zeros((slab_rows, col_loc), jnp.float32)
            .at[:, col_table[child]]
            .add(landed[child], mode="drop")
        )
        assembled = assembled.at[row_dest[child]].add(spread, mode="drop")
    width = inverse_blocks.shape[1]
    count = inverse_blocks.shape[0]
    span = n_col // groups
    root = my_col // span
    factors = []
    tops = []
    for block in range(count):
        current = assembled[:, block * width : (block + 1) * width]
        if block > 0:
            earlier = jnp.concatenate(factors, axis=1)
            above = jnp.concatenate(
                [
                    tops[prior][(block - prior - 1) * width : (block - prior) * width]
                    for prior in range(block)
                ],
                axis=1,
            )
            current = current - highest_outer(earlier, above)
        result = highest_outer(current, jnp.tril(inverse_blocks[block]))
        factors.append(result)
        if block + 1 < count:
            tops.append(from_root(result[(block + 1) * width : count * width], ("half", "row"), 0))
    local_factor = jnp.concatenate(factors, axis=1)
    factor_rows = from_root(local_factor, "col", 0)
    factor_cols = from_root(factor_rows, ("half", "row"), root)
    updated_front = assembled - highest_outer(factor_rows, factor_cols)
    return (updated_front, factor_rows.astype(jnp.bfloat16))


def solution(mesh):
    in_specs = (P(("half", "row"), "col"), P("half", "row", "col"), P(), P())
    out_specs = (P(("half", "row"), "col"), P(("half", "row"), None))
    return jax.shard_map(local, mesh=mesh, in_specs=in_specs, out_specs=out_specs, check_vma=False)
```

profile of v0, /device:TPU:1, one launch (start us, length us, event | category | flops | bytes accessed | tf_op | source)
XLA Modules:
  0.0 1522.6 jit_solution(5224957147716496916)
XLA Ops:
  7.2 5.0 copy.95
  13.4 123.6 %reduce-window.14 = s32[16,16,8,128]{3,2,1,0:T(8,128)S(1)} reduce-window(s32[16,16,8,128]{3,2,1,0:T(8,128)} %fusion.34, s32[]{:T(128)} %constant.102.clone.1), window={size=1x1x1x128 pad=0_0x0_0x0_0x127_0}, to_apply=%region_0.1 | reduce-window | flops 33292288 | bytes 2097156 | tf_op jit(solution)/shard_map/reduce-window
  143.6 7.1 scatter_custom_fusion.1
  150.7 12.4 all-to-all-start
  163.5 36.3 %reduce-window.16 = s32[2,16,16,4,128]{4,2,3,1,0:T(8,128)S(1)} reduce-window(s32[2,16,16,4,128]{4,2,3,1,0:T(8,128)S(1)} %fusion.35, s32[]{:T(128)} %constant.102.clone.1), window={size=1x1x1x1x128 pad=0_0x0_0x0_0x0_0x127_0}, to_apply=%region_4.5 | reduce-window | flops 33292288 | bytes 2097156 | tf_op jit(solution)/shard_map/reduce-window.2
  201.9 59.7 %all-to-all-done = f32[16,128,512]{2,1,0:T(8,128)} async-done(((f32[16,128,512]{2,1,0:T(8,128)}), f32[16,128,512]{2,1,0:T(8,128)}, u32[]{:S(2)}, u32[]{:S(2)}) %all-to-all-start) | async-done | bytes 4194336 | tf_op jit(solution)/shard_map/all_to_all | solution.py:83
  261.6 4.2 fusion.82
  269.5 5.7 scatter_custom_fusion.2
  275.2 4.6 scatter_custom_fusion.3
  279.8 4.3 pad_maximum_fusion
  284.1 13.0 copy.34
  297.1 5.8 all-to-all-start.1
  303.7 60.3 %scatter_custom_fusion.8 = s32[2048]{0:T(1024)S(1)} fusion(s32[16384]{0:T(1024)S(1)} %bitcast.176, s32[16384]{0:T(1024)S(1)} %bitcast.177, s32[]{:T(128)} %constant.100.clone.1), kind=kCustom, calls=%fused_computation.152 | custom fusion | bytes 8196
  364.5 60.5 %scatter_custom_fusion = s32[2048]{0:T(1024)S(1)} fusion(s32[16384]{0:T(1024)S(1)} %bitcast.175, s32[16384]{0:T(1024)S(1)} %add_select_fusion.4, s32[]{:T(128)} %constant.100.clone.1), kind=kCustom, calls=%fused_computation.154 | custom fusion | bytes 8196 | tf_op jit(solution)/shard_map/scatter | solution.py:37
  425.0 63.9 %all-to-all-done.1 = f32[2,1024,1024]{1,0,2:T(2,128)} async-done(((f32[2,1024,1024]{1,0,2:T(2,128)}), f32[2,1024,1024]{1,0,2:T(2,128)}, u32[]{:S(2)}, u32[]{:S(2)}) %all-to-all-start.1) | async-done | bytes 8388640 | tf_op jit(solution)/shard_map/all_to_all | solution.py:89
  489.0 11.6 fusion.81
  500.5 13.6 scatter_custom_fusion.4
  514.1 5.3 copy.35
  519.5 14.0 scatter_custom_fusion.6
  533.4 5.3 copy.36
  538.8 14.4 scatter_fusion
  553.2 14.4 scatter_fusion.1
  570.3 174.1 %all-reduce.6.cloned.1.call-done = f32[384,128]{0,1:T(8,128)} async-done(((f32[384,128]{0,1:T(8,128)}), f32[384,128]{0,1:T(8,128)}) %all-reduce.6.cloned.1.call-update) | async-done | bytes 196624 | tf_op jit(solution)/shard_map/psum | solution.py:9
  744.4 2.1 convolution_subtract_fusion.2
  748.8 184.5 %all-reduce.8.cloned.1.call-done = f32[256,128]{0,1:T(8,128)} async-done(((f32[256,128]{0,1:T(8,128)}), f32[256,128]{0,1:T(8,128)}) %all-reduce.8.cloned.1.call-update) | async-done | bytes 131088 | tf_op jit(solution)/shard_map/psum | solution.py:9
  934.2 2.9 convolution_subtract_fusion.1
  938.6 177.9 %all-reduce.10.cloned.1.call-done = f32[128,128]{0,1:T(8,128)} async-done(((f32[128,128]{0,1:T(8,128)}), f32[128,128]{0,1:T(8,128)}) %all-reduce.10.cloned.1.call-update) | async-done | bytes 65552 | tf_op jit(solution)/shard_map/psum | solution.py:9
  1116.5 3.8 fusion.23
  1122.6 166.6 %all-reduce.12.cloned.1.call-done = f32[1024,512]{0,1:T(8,128)} async-done(((f32[1024,512]{0,1:T(8,128)}), f32[1024,512]{0,1:T(8,128)}) %all-reduce.12.cloned.1.call-update) | async-done | bytes 2097168 | tf_op jit(solution)/shard_map/psum | solution.py:9
  1289.2 4.1 fusion.83
  1294.6 210.5 %all-reduce.14.cloned.1.call-done = f32[1024,512]{0,1:T(8,128)} async-done(((f32[1024,512]{0,1:T(8,128)}), f32[1024,512]{0,1:T(8,128)}) %all-reduce.14.cloned.1.call-update) | async-done | bytes 2097168 | tf_op jit(solution)/shard_map/psum | solution.py:9
  1505.1 10.8 convolution_subtract_fusion
  (85 shorter events, 26.0 us)
Async XLA Ops:
  7.2 136.5 %copy-start = (f32[1,1024,512]{2,1,0:T(8,128)S(1)}, f32[1,1024,512]{2,1,0:T(8,128)}, u32[]{:S(2)}) copy-start(f32[1,1024,512]{2,1,0:T(8,128)} %param.5) | copy-start | bytes 6291460
  7.2 5.0 copy-start.2
  150.7 110.8 %all-to-all-start = ((f32[16,128,512]{2,1,0:T(8,128)}), f32[16,128,512]{2,1,0:T(8,128)}, u32[]{:S(2)}, u32[]{:S(2)}) async-start(f32[16,128,512]{2,1,0:T(8,128)} %bitcast.160), calls=%async_computation | async-start | bytes 8388608 | tf_op jit(solution)/shard_map/all_to_all | solution.py:83
  297.1 6.0 copy-start.5
  297.1 6.1 copy-start.4
  297.1 6.5 copy-start.3
  297.1 191.9 %all-to-all-start.1 = ((f32[2,1024,1024]{1,0,2:T(2,128)}), f32[2,1024,1024]{1,0,2:T(2,128)}, u32[]{:S(2)}, u32[]{:S(2)}) async-start(f32[2,1024,1024]{1,0,2:T(2,128)} %copy.34), calls=%async_computation.1 | async-start | bytes 16777216 | tf_op jit(solution)/shard_map/all_to_all | solution.py:89
  302.9 441.5 %all-reduce.6.cloned.1.call-start = ((), (), s32[]{:S(2)}) async-start(), calls=%async_computation.2 | async-start | bytes 393216 | tf_op jit(solution)/shard_map/psum | solution.py:9
  570.1 363.2 %all-reduce.8.cloned.1.call-start = ((), (), s32[]{:S(2)}) async-start(), calls=%async_computation.3 | async-start | bytes 262144 | tf_op jit(solution)/shard_map/psum | solution.py:9
  747.8 368.7 %all-reduce.10.cloned.1.call-start = ((), (), s32[]{:S(2)}) async-start(), calls=%async_computation.4 | async-start | bytes 131072 | tf_op jit(solution)/shard_map/psum | solution.py:9
  938.3 350.9 %all-reduce.12.cloned.1.call-start = ((), (), s32[]{:S(2)}) async-start(), calls=%async_computation.5 | async-start | bytes 4194304 | tf_op jit(solution)/shard_map/psum | solution.py:9
  1122.6 382.5 %all-reduce.14.cloned.1.call-start = ((), (), s32[]{:S(2)}) async-start(), calls=%async_computation.6 | async-start | bytes 4194304 | tf_op jit(solution)/shard_map/psum | solution.py:9
  1293.3 222.6 %copy-start.1 = (f32[1,1024,512]{2,1,0:T(8,128)S(1)}, f32[1,1024,512]{2,1,0:T(8,128)}, u32[]{:S(2)}) copy-start(f32[1,1024,512]{2,1,0:T(8,128)} %param.5) | copy-start | bytes 6291460
Sparse Core Ops, SparseCore 0:
  570.2 174.1 all-reduce.5
  748.0 185.2 all-reduce.7
  938.4 178.0 all-reduce.9
  1122.7 166.4 all-reduce.11
  1293.4 211.6 all-reduce.13
where the time goes:
time: 1540 us; the launch traced here: 1520 us
  waiting for transfers between devices  1040 us (68%)
  other arithmetic  233 us (15%)
  local copies, waits for them, and re-layouts  196 us (13%)
  matrix products  23.1 us (2%)
  starting transfers between devices  18.6 us (1%)
    psum x5, waiting for transfers between devices, from_root(): return lax.psum(block, axis)  913 us
    another operation x5, other arithmetic  161 us
    unnamed x24, local copies, waits for them, and re-layouts  67.2 us
    all_to_all x1, waiting for transfers between devices, local(): lax.all_to_all(outgoing, 'col', split_axis=2, concat_axis=2, tiled=True)  63.9 us
    scatter x1, local copies, waits for them, and re-layouts, row_tables(): table = jnp.full((groups * cap_rows,), row_loc, jnp.int32).at[where_at.re...  60.5 us
    all_to_all x1, waiting for transfers between devices, local(): lax.all_to_all(moved, ('half', 'row'), split_axis=0, concat_axis=0, tiled...  59.7 us
  transfers between devices with their start and end apart: 7, of which 7 were waited for; matrix products, arithmetic and copies ran while one was open for 11% of the time, Pallas kernels for 0%

commit v1 on v0

--- a/solution.py
+++ b/solution.py
@@ -6,7 +6,7 @@
 
 def from_root(block, axis, holder):
     block = jnp.where(lax.axis_index(axis) == holder, block, jnp.zeros_like(block))
-    return lax.psum(block, axis)
+    return jnp.sum(lax.all_gather(block, axis), axis=0)
 
 
 def highest_outer(left, right):

time: 1540 us -> 1860 us (1.21)
  waiting for transfers between devices: 1040 us -> 1290 us
  local copies, waits for them, and re-layouts: 196 us -> 240 us
  other arithmetic: 233 us -> 256 us
    all_gather x0 -> x5, waiting for transfers between devices: none -> 1170 us  [from_root(): return jnp.sum(lax.all_gather(block, axis), axis=0)]
    psum x5 -> x0, waiting for transfers between devices: 913 us -> none  [from_root(): return lax.psum(block, axis)]
    unnamed x24 -> x33, local copies, waits for them, and re-layouts: 67.2 us -> 108 us
  transfers between devices with their start and end apart: 7 -> 7, of which waited for: 7 -> 7; matrix products, arithmetic and copies ran while one was open for 11% -> 9% of each run, Pallas kernels for 0% -> 0%
where the time goes in v1:
time: 1860 us; the launch traced here: 1850 us
  waiting for transfers between devices  1290 us (69%)
  other arithmetic  256 us (14%)
  local copies, waits for them, and re-layouts  240 us (13%)
  matrix products  22.4 us (1%)
  starting transfers between devices  18.9 us (1%)
    all_gather x5, waiting for transfers between devices, from_root(): return jnp.sum(lax.all_gather(block, axis), axis=0)  1170 us
    another operation x5, other arithmetic  161 us
    unnamed x33, local copies, waits for them, and re-layouts  108 us
    all_to_all x1, waiting for transfers between devices, local(): lax.all_to_all(outgoing, 'col', split_axis=2, concat_axis=2, tiled=True)  63.7 us
    scatter x1, local copies, waits for them, and re-layouts, row_tables(): table = jnp.full((groups * cap_rows,), row_loc, jnp.int32).at[where_at.re...  60.3 us
    all_to_all x1, waiting for transfers between devices, local(): lax.all_to_all(moved, ('half', 'row'), split_axis=0, concat_axis=0, tiled...  59.7 us
  transfers between devices with their start and end apart: 7, of which 7 were waited for; matrix products, arithmetic and copies ran while one was open for 9% of the time, Pallas kernels for 0%

profile of v1, /device:TPU:1, one launch (start us, length us, event | category | flops | bytes accessed | tf_op | source)
XLA Modules:
  0.0 1845.7 jit_solution(3631280965518503939)
XLA Ops:
  7.2 5.0 copy.112
  13.5 123.6 %reduce-window.14 = s32[16,16,8,128]{3,2,1,0:T(8,128)S(1)} reduce-window(s32[16,16,8,128]{3,2,1,0:T(8,128)} %fusion.34, s32[]{:T(128)} %constant.103.clone.1), window={size=1x1x1x128 pad=0_0x0_0x0_0x127_0}, to_apply=%region_0.1 | reduce-window | flops 33292288 | bytes 2097156 | tf_op jit(solution)/shard_map/reduce-window
  143.6 7.1 scatter_custom_fusion.1
  150.7 12.4 all-to-all-start
  163.5 36.3 %reduce-window.16 = s32[2,16,16,4,128]{4,2,3,1,0:T(8,128)S(1)} reduce-window(s32[2,16,16,4,128]{4,2,3,1,0:T(8,128)S(1)} %fusion.35, s32[]{:T(128)} %constant.103.clone.1), window={size=1x1x1x1x128 pad=0_0x0_0x0_0x0_0x127_0}, to_apply=%region_4.5 | reduce-window | flops 33292288 | bytes 2097156 | tf_op jit(solution)/shard_map/reduce-window.2
  201.9 59.7 %all-to-all-done = f32[16,128,512]{2,1,0:T(8,128)} async-done(((f32[16,128,512]{2,1,0:T(8,128)}), f32[16,128,512]{2,1,0:T(8,128)}, u32[]{:S(2)}, u32[]{:S(2)}) %all-to-all-start) | async-done | bytes 4194336 | tf_op jit(solution)/shard_map/all_to_all | solution.py:83
  261.6 4.8 fusion.81
  271.2 5.7 scatter_custom_fusion.3
  277.0 4.6 scatter_custom_fusion.2
  281.6 4.3 pad_maximum_fusion
  285.9 13.0 copy.49
  298.9 5.8 all-to-all-start.1
  305.9 60.3 %scatter_custom_fusion = s32[2048]{0:T(1024)S(1)} fusion(s32[16384]{0:T(1024)S(1)} %bitcast.212, s32[16384]{0:T(1024)S(1)} %add_select_fusion.4, s32[]{:T(128)} %constant.101.clone.1), kind=kCustom, calls=%fused_computation.158 | custom fusion | bytes 8196 | tf_op jit(solution)/shard_map/scatter | solution.py:37
  366.2 60.7 %scatter_custom_fusion.8 = s32[2048]{0:T(1024)S(1)} fusion(s32[16384]{0:T(1024)S(1)} %bitcast.214, s32[16384]{0:T(1024)S(1)} %bitcast.213, s32[]{:T(128)} %constant.101.clone.1), kind=kCustom, calls=%fused_computation.156 | custom fusion | bytes 8196
  427.0 63.7 %all-to-all-done.1 = f32[2,1024,1024]{1,0,2:T(2,128)} async-done(((f32[2,1024,1024]{1,0,2:T(2,128)}), f32[2,1024,1024]{1,0,2:T(2,128)}, u32[]{:S(2)}, u32[]{:S(2)}) %all-to-all-start.1) | async-done | bytes 8388640 | tf_op jit(solution)/shard_map/all_to_all | solution.py:89
  490.8 11.6 fusion.80
  502.3 13.6 scatter_custom_fusion.6
  515.9 5.3 copy.51
  521.2 13.7 scatter_custom_fusion.4
  535.0 5.3 copy.50
  540.3 14.4 scatter_fusion
  554.8 14.4 scatter_fusion.1
  571.8 64.5 %all-gather.12.cloned.1.call-done = f32[6144,128]{0,1:T(8,128)} async-done(((f32[384,128]{0,1:T(8,128)}), f32[6144,128]{0,1:T(8,128)}) %all-gather.12.cloned.1.call-update) | async-done | bytes 3145744 | tf_op jit(solution)/shard_map/all_gather | solution.py:9
  643.0 58.6 %all-gather.14.cloned.1.call-done = f32[4096,128]{0,1:T(8,128)} async-done(((f32[256,128]{0,1:T(8,128)}), f32[4096,128]{0,1:T(8,128)}) %all-gather.14.cloned.1.call-update) | async-done | bytes 2097168 | tf_op jit(solution)/shard_map/all_gather | solution.py:9
  708.5 51.6 %all-gather.16.cloned.1.call-done = f32[2048,128]{0,1:T(8,128)} async-done(((f32[128,128]{0,1:T(8,128)}), f32[2048,128]{0,1:T(8,128)}) %all-gather.16.cloned.1.call-update) | async-done | bytes 1048592 | tf_op jit(solution)/shard_map/all_gather | solution.py:9
  771.0 684.4 %all-gather.10.cloned.1.call-done = f32[16,1024,512]{2,1,0:T(8,128)} async-done(((f32[1,1024,512]{2,1,0:T(8,128)}), f32[16,1024,512]{2,1,0:T(8,128)}) %all-gather.10.cloned.1.call-update) | async-done | bytes 33554448 | tf_op jit(solution)/shard_map/all_gather | solution.py:9
  1455.5 12.7 reduce_sum.71
  1470.2 4.1 fusion.82
  1475.7 310.6 %all-gather.18.cloned.1.call-done = f32[16384,512]{0,1:T(8,128)} async-done(((f32[1024,512]{0,1:T(8,128)}), f32[16384,512]{0,1:T(8,128)}) %all-gather.18.cloned.1.call-update) | async-done | bytes 33554448 | tf_op jit(solution)/shard_map/all_gather | solution.py:9
  1786.3 32.5 %copy.79 = f32[64,8,16,1024]{3,2,1,0:T(8,128)S(1)} copy(f32[64,8,16,1024]{3,1,2,0:T(8,128)} %bitcast.190) | data formatting | bytes 67108864
  1818.8 9.7 bitcast_reduce_fusion
  1828.6 10.1 convolution_subtract_fusion
  (99 shorter events, 46.4 us)
Async XLA Ops:
  7.2 136.5 %copy-start = (f32[1,1024,512]{2,1,0:T(8,128)S(1)}, f32[1,1024,512]{2,1,0:T(8,128)}, u32[]{:S(2)}) copy-start(f32[1,1024,512]{2,1,0:T(8,128)} %param.5) | copy-start | bytes 6291460
  7.2 5.0 copy-start.4
  150.7 110.8 %all-to-all-start = ((f32[16,128,512]{2,1,0:T(8,128)}), f32[16,128,512]{2,1,0:T(8,128)}, u32[]{:S(2)}, u32[]{:S(2)}) async-start(f32[16,128,512]{2,1,0:T(8,128)} %bitcast.191), calls=%async_computation | async-start | bytes 8388608 | tf_op jit(solution)/shard_map/all_to_all | solution.py:83
  298.8 6.0 copy-start.5
  298.8 6.4 copy-start.7
  298.9 6.5 copy-start.6
  298.9 191.9 %all-to-all-start.1 = ((f32[2,1024,1024]{1,0,2:T(2,128)}), f32[2,1024,1024]{1,0,2:T(2,128)}, u32[]{:S(2)}, u32[]{:S(2)}) async-start(f32[2,1024,1024]{1,0,2:T(2,128)} %copy.49), calls=%async_computation.1 | async-start | bytes 16777216 | tf_op jit(solution)/shard_map/all_to_all | solution.py:89
  304.7 331.6 %all-gather.12.cloned.1.call-start = ((), (), s32[]{:S(2)}) async-start(), calls=%async_computation.3 | async-start | bytes 3342336 | tf_op jit(solution)/shard_map/all_gather | solution.py:9
  571.6 130.0 %all-gather.14.cloned.1.call-start = ((), (), s32[]{:S(2)}) async-start(), calls=%async_computation.4 | async-start | bytes 2228224 | tf_op jit(solution)/shard_map/all_gather | solution.py:9
  642.6 117.5 %all-gather.16.cloned.1.call-start = ((), (), s32[]{:S(2)}) async-start(), calls=%async_computation.5 | async-start | bytes 1114112 | tf_op jit(solution)/shard_map/all_gather | solution.py:9
  708.4 747.1 %all-gather.10.cloned.1.call-start = ((), (), s32[]{:S(2)}) async-start(), calls=%async_computation.2 | async-start | bytes 35651584 | tf_op jit(solution)/shard_map/all_gather | solution.py:9
  770.7 1015.6 %all-gather.18.cloned.1.call-start = ((), (), s32[]{:S(2)}) async-start(), calls=%async_computation.6 | async-start | bytes 35651584 | tf_op jit(solution)/shard_map/all_gather | solution.py:9
  1468.2 6.2 copy-start.3
  1818.8 9.8 copy-start.2
  1818.8 19.9 %copy-start.1 = (f32[1,1024,512]{2,1,0:T(8,128)S(1)}, f32[1,1024,512]{2,1,0:T(8,128)}, u32[]{:S(2)}) copy-start(f32[1,1024,512]{2,1,0:T(8,128)} %param.5) | copy-start | bytes 6291460
Sparse Core Ops, SparseCore 0:
  571.7 64.4 all-gather.11
  642.7 58.8 all-gather.13
  708.5 51.5 all-gather.15
  770.8 684.5 all-gather.9
  1474.5 311.7 all-gather.17
